TPU v7x, 32 devices: a whole 2x2x4 slice. The times are simulated.
32 devices in a mesh: runs: 2 (over x), tm: 16 (over z, y, core), pix: 1.
Axes of the slice: x: 2, y: 2, z: 4, core: 2. Of those that a mesh axis runs over, the one named last changes fastest.
Arguments:
- intensity: float32 [2048, 4096], P('tm', ('runs', 'pix')), parts along dimension 1, may hold values from 0.01 to 60
- cycle_label: int32 [4096], P(('runs', 'pix')), parts along dimension 0, may hold values from 0 to 127, as said below
- valid_mask: int32 [4096], P(('runs', 'pix')), parts along dimension 0, may hold values from 0 to 1, as said below
Outputs:
- correlation: float32 [128, 4096], P('tm', ('runs', 'pix')), parts along dimension 1
There are 2 independent parts, one for each index of `runs`. A program takes and returns all parts, laid end to end along the dimension named above; each array names one. Nothing has to cross between parts.
Inputs may be any that keep to these rules, and one draw needn't show every extreme that they name: `cycle_label`: every cycle 0 to 127 is the label of exactly 16 pixels. `valid_mask`: every cycle holds at least one pixel marked 1.
All inputs are finite; a program needn't handle non-finite values.
Results may differ from a plain program's by a relative error of at most 0.0001.
Values sent between devices are 32-bit elements; how exact they have to be, the bound alone decides.
A program may use at most 64 MiB of HBM per device.

v0:
```python
import jax
import jax.numpy as jnp
from jax import lax
from jax.sharding import PartitionSpec as P

Q = 128
LEVELS = 8
LAGS = 16


def coarsen(series):
    paired = series.reshape(series.shape[0] // 2, 2, series.shape[1])
    return (paired[:, 0] + paired[:, 1]) * 0.5


def level_rows(series, extension, total_frames):
    frames_here = series.shape[0]
    row_list = []
    for offset in range(extension.shape[0] + 1):
        inside = min(offset, frames_here)
        total = jnp.sum(series[: frames_here - inside] * series[inside:], axis=0)
        if offset > 0:
            tail_rows = series[frames_here - inside :]
            total = total + jnp.sum(tail_rows * extension[offset - inside : offset], axis=0)
        row_list.append(total / (total_frames - offset))
    return row_list


def pixel_rows(gathered):
    series = gathered[:, 0, :]
    row_list = []
    for height in range(LEVELS):
        if height > 0:
            series = coarsen(series)
        extension = jnp.zeros((LAGS - 1, series.shape[1]), jnp.float32)
        row_list = row_list + level_rows(series, extension, series.shape[0])
    return jnp.stack(row_list)


def body(intensity, cycle_label, valid_mask):
    valid_flag = valid_mask.astype(jnp.float32)
    member = (cycle_label[:, None] == jnp.arange(Q, dtype=jnp.int32)[None, :]).astype(jnp.float32)
    weighted = member * valid_flag[:, None]
    partial_sum = jnp.dot(intensity, weighted, precision=lax.Precision.HIGHEST)
    partial_count = jnp.sum(weighted, axis=0)
    cycle_sum, cycle_count = lax.psum((partial_sum, partial_count), "pix")
    cycle_mean = cycle_sum / cycle_count[None, :]
    per_pixel = lax.dot_general(
        cycle_mean, member, (((1,), (1,)), ((), ())), precision=lax.Precision.HIGHEST
    )
    normed = valid_flag[None, :] * intensity / per_pixel
    devices_tm = lax.axis_size("tm")
    tile_width = normed.shape[1] // devices_tm
    pieces = normed.reshape(normed.shape[0], devices_tm, tile_width)
    rows_local = pixel_rows(lax.all_to_all(pieces, "tm", split_axis=1, concat_axis=0, tiled=True))
    return lax.all_to_all(rows_local, "tm", split_axis=0, concat_axis=1, tiled=True)


def solution(mesh):
    placed = (P("tm", ("runs", "pix")), P(("runs", "pix")), P(("runs", "pix")))
    return jax.shard_map(
        body, mesh=mesh, in_specs=placed, out_specs=P("tm", ("runs", "pix")), check_vma=False
    )
```

profile of v0, /device:TPU:0, one launch (start us, length us, event | category | flops | bytes accessed | tf_op | source)
XLA Modules:
  0.0 95.0 jit_solution(12186441031817750926)
XLA Ops:
  0.0 0.8 convert_element_type.4
  0.8 0.7 select_reduce_fusion
  1.5 3.6 %fusion.3 = f32[128,128]{1,0:T(8,128)S(1)} fusion(f32[128,2048]{1,0:T(8,128)} %param.3, f32[2048]{0:T(1024)S(1)} %convert_element_type.4, s32[2048]{0:T(1024)S(1)} %copy-done, f32[128]{0:T(128)S(1)} %select_reduce_fusion), kind=kOutput, calls=%fused_computation.5 | convolution fusion | flops 403193856 | bytes 1131008 | tf_op jit(solution)/shard_map/dot_general | solution.py:44
  5.1 1.2 %fusion.2 = f32[16,16,8,128]{3,2,1,0:T(8,128)S(1)} fusion(f32[128,128]{1,0:T(8,128)S(1)} %fusion.3, f32[128,2048]{1,0:T(8,128)S(1)} %copy-done.1, s32[2048]{0:T(1024)S(1)} %copy-done, f32[2048]{0:T(1024)S(1)} %convert_element_type.4), kind=kOutput, calls=%fused_computation.4 | convolution fusion | flops 403439616 | bytes 2179072 | tf_op jit(solution)/shard_map/dot_general | solution.py:48
  6.5 31.9 %all_to_all.34 = f32[128,16,128]{2,0,1:T(8,128)S(1)} all-to-all(f32[128,16,128]{2,0,1:T(8,128)S(1)} %bitcast.378), channel_id=1, replica_groups=mesh['runs'=2,'tm'=16,'pix'=1] {'tm'}, dimensions={1} | all-to-all | bytes 2097152 | tf_op jit(solution)/shard_map/all_to_all | solution.py:55
  40.2 0.3 fusion.7
  40.8 0.3 fusion.8
  41.4 0.3 fusion.9
  41.8 0.3 fusion.10
  42.4 0.3 fusion.11
  42.7 0.3 fusion.12
  43.0 1.2 %multiply_reduce_fusion = (f32[128]{0:T(128)S(1)}, f32[1024,1,128]{2,1,0:T(1,128)S(1)}) fusion(f32[1024,2,128]{2,1,0:T(2,128)S(1)} %bitcast.370), kind=kLoop, calls=%fused_computation.42 | loop fusion | flops 524160 | bytes 1573376 | tf_op jit(solution)/shard_map/reduce_sum | solution.py:21
  44.2 1.1 %fusion.36 = f32[128]{0:T(128)S(1)} fusion(f32[1024,1,128]{2,1,0:T(1,128)S(1)} %get-tuple-element.46), kind=kLoop, calls=%fused_computation.66 | loop fusion | flops 259456 | bytes 1038848 | tf_op jit(solution)/shard_map/reduce_sum | solution.py:21
  45.3 1.1 %fusion.38 = f32[128]{0:T(128)S(1)} fusion(f32[1024,1,128]{2,1,0:T(1,128)S(1)} %get-tuple-element.46), kind=kLoop, calls=%fused_computation.70 | loop fusion | flops 258944 | bytes 1036800 | tf_op jit(solution)/shard_map/reduce_sum | solution.py:21
  46.4 1.1 %fusion.35 = f32[128]{0:T(128)S(1)} fusion(f32[1024,1,128]{2,1,0:T(1,128)S(1)} %get-tuple-element.46), kind=kLoop, calls=%fused_computation.64 | loop fusion | flops 259712 | bytes 1039872 | tf_op jit(solution)/shard_map/reduce_sum | solution.py:21
  47.5 1.1 %fusion.39 = f32[128]{0:T(128)S(1)} fusion(f32[1024,1,128]{2,1,0:T(1,128)S(1)} %get-tuple-element.46), kind=kLoop, calls=%fused_computation.72 | loop fusion | flops 258688 | bytes 1035776 | tf_op jit(solution)/shard_map/reduce_sum | solution.py:21
  48.6 1.1 %fusion.34 = f32[128]{0:T(128)S(1)} fusion(f32[1024,1,128]{2,1,0:T(1,128)S(1)} %get-tuple-element.46), kind=kLoop, calls=%fused_computation.62 | loop fusion | flops 259968 | bytes 1040896 | tf_op jit(solution)/shard_map/reduce_sum | solution.py:21
  49.8 1.1 %fusion.33 = f32[128]{0:T(128)S(1)} fusion(f32[1024,1,128]{2,1,0:T(1,128)S(1)} %get-tuple-element.46), kind=kLoop, calls=%fused_computation.60 | loop fusion | flops 260224 | bytes 1041920 | tf_op jit(solution)/shard_map/reduce_sum | solution.py:21
  50.9 1.1 %fusion.32 = f32[128]{0:T(128)S(1)} fusion(f32[1024,1,128]{2,1,0:T(1,128)S(1)} %get-tuple-element.46), kind=kLoop, calls=%fused_computation.58 | loop fusion | flops 260480 | bytes 1042944 | tf_op jit(solution)/shard_map/reduce_sum | solution.py:21
  52.0 1.1 %fusion.40 = f32[128]{0:T(128)S(1)} fusion(f32[1024,1,128]{2,1,0:T(1,128)S(1)} %get-tuple-element.46), kind=kLoop, calls=%fused_computation.74 | loop fusion | flops 258432 | bytes 1034752 | tf_op jit(solution)/shard_map/reduce_sum | solution.py:21
  53.1 1.1 %fusion.31 = f32[128]{0:T(128)S(1)} fusion(f32[1024,1,128]{2,1,0:T(1,128)S(1)} %get-tuple-element.46), kind=kLoop, calls=%fused_computation.56 | loop fusion | flops 260736 | bytes 1043968 | tf_op jit(solution)/shard_map/reduce_sum | solution.py:21
  54.2 1.1 %fusion.30 = f32[128]{0:T(128)S(1)} fusion(f32[1024,1,128]{2,1,0:T(1,128)S(1)} %get-tuple-element.46), kind=kLoop, calls=%fused_computation.54 | loop fusion | flops 260992 | bytes 1044992 | tf_op jit(solution)/shard_map/reduce_sum | solution.py:21
  55.3 1.3 %fusion.37 = f32[128]{0:T(128)S(1)} fusion(f32[1024,1,128]{2,1,0:T(1,128)S(1)} %get-tuple-element.46), kind=kLoop, calls=%fused_computation.68 | loop fusion | flops 259200 | bytes 1037824 | tf_op jit(solution)/shard_map/reduce_sum | solution.py:21
  56.6 1.1 %fusion.29 = f32[128]{0:T(128)S(1)} fusion(f32[1024,1,128]{2,1,0:T(1,128)S(1)} %get-tuple-element.46), kind=kLoop, calls=%fused_computation.52 | loop fusion | flops 261248 | bytes 1046016 | tf_op jit(solution)/shard_map/reduce_sum | solution.py:21
  57.7 1.1 %fusion.41 = f32[128]{0:T(128)S(1)} fusion(f32[1024,1,128]{2,1,0:T(1,128)S(1)} %get-tuple-element.46), kind=kLoop, calls=%fused_computation.76 | loop fusion | flops 258176 | bytes 1033728 | tf_op jit(solution)/shard_map/reduce_sum | solution.py:21
  58.8 1.1 %fusion.28 = f32[128]{0:T(128)S(1)} fusion(f32[1024,1,128]{2,1,0:T(1,128)S(1)} %get-tuple-element.46), kind=kLoop, calls=%fused_computation.50 | loop fusion | flops 261504 | bytes 1047040 | tf_op jit(solution)/shard_map/reduce_sum | solution.py:21
  60.0 1.1 %fusion.27 = f32[128]{0:T(128)S(1)} fusion(f32[1024,1,128]{2,1,0:T(1,128)S(1)} %get-tuple-element.46), kind=kLoop, calls=%fused_computation.48 | loop fusion | flops 261760 | bytes 1048064 | tf_op jit(solution)/shard_map/reduce_sum | solution.py:21
  61.1 0.6 multiply_reduce_fusion.1
  61.7 0.5 fusion.52
  62.2 0.5 fusion.54
  62.8 0.5 fusion.51
  63.4 0.5 fusion.55
  63.9 0.5 fusion.50
  64.5 0.5 fusion.49
  65.1 0.5 fusion.48
  65.7 0.5 fusion.56
  66.2 0.6 fusion.47
  66.9 0.6 fusion.46
  67.4 0.5 fusion.53
  68.0 0.6 fusion.45
  68.5 0.5 fusion.57
  69.1 0.6 fusion.44
  69.7 0.6 fusion.43
  70.3 0.3 multiply_reduce_fusion.2
  75.6 0.4 fusion.83
  82.3 0.4 stack.2
  82.6 11.7 %all_to_all.35 = f32[16,8,128]{2,1,0:T(8,128)S(1)} all-to-all(f32[16,8,128]{2,1,0:T(8,128)S(1)} %bitcast.379), channel_id=1, replica_groups=mesh['runs'=2,'tm'=16,'pix'=1] {'tm'}, dimensions={0} | all-to-all | bytes 131072 | tf_op jit(solution)/shard_map/all_to_all | solution.py:56
  94.4 0.6 copy.12
  (254 shorter events, 14.5 us)
Async XLA Ops:
  0.0 0.8 copy-start
  0.0 5.1 %copy-start.1 = (f32[128,2048]{1,0:T(8,128)S(1)}, f32[128,2048]{1,0:T(8,128)}, u32[]{:S(2)}) copy-start(f32[128,2048]{1,0:T(8,128)} %param.3) | copy-start | bytes 3145732
where the time goes:
time: 95.3 us; the launch traced here: 95 us
  other arithmetic  44.8 us (47%)
  blocking collectives  43.6 us (46%)
  matrix products  4.86 us (5%)
  local copies, waits for them, and re-layouts  1.1 us (1%)
    reduce_sum x119, other arithmetic, level_rows(): total = jnp.sum(series[:frames_here - inside] * series[inside:], axis=0)  40.1 us
    all_to_all x1, blocking collectives, body(): lax.all_to_all(pieces, 'tm', split_axis=1, concat_axis=0, tiled=True)  31.9 us
    all_to_all x1, blocking collectives, body(): lax.all_to_all(rows_local, 'tm', split_axis=0, concat_axis=1, tiled=True)  11.7 us
    dot_general x1, matrix products, body(): partial_sum = jnp.dot(intensity, weighted, precision=lax.Precision.HIGHEST)  3.63 us
    reduce_sum x106, other arithmetic, level_rows(): jnp.sum(tail_rows * extension[offset - inside:offset], axis=0)  2.74 us

commit v1 on v0

--- a/solution.py
+++ b/solution.py
@@ -1,6 +1,9 @@
+import functools
 import jax
 import jax.numpy as jnp
 from jax import lax
+from jax.experimental import pallas as pl
+from jax.experimental.pallas import tpu as pltpu
 from jax.sharding import PartitionSpec as P
 
 Q = 128
@@ -55,9 +58,329 @@
     rows_local = pixel_rows(lax.all_to_all(pieces, "tm", split_axis=1, concat_axis=0, tiled=True))
     return lax.all_to_all(rows_local, "tm", split_axis=0, concat_axis=1, tiled=True)
 
+LOCAL = 3
+LANES = 128
+SUB = 8
+
+
+def split3(x):
+    high = x.astype(jnp.bfloat16)
+    rest = x - high.astype(jnp.float32)
+    mid = rest.astype(jnp.bfloat16)
+    low = (rest - mid.astype(jnp.float32)).astype(jnp.bfloat16)
+    return high, mid, low
+
+
+def fold_rows(parts):
+    row = lax.broadcasted_iota(jnp.int32, (SUB, LANES), 0)
+    for step in (4, 2, 1):
+        keep = (row & step) == 0
+
+        def swap(v, step=step, keep=keep):
+            if step == 4:
+                return pltpu.roll(v, 4, 0)
+            return jnp.where(keep, pltpu.roll(v, SUB - step, 0), pltpu.roll(v, step, 0))
+
+        parts = [
+            jnp.where(keep, parts[i], parts[i + step]) + swap(jnp.where(keep, parts[i + step], parts[i]))
+            for i in range(step)
+        ]
+    return parts[0]
+
+
+def add_lags(ref, c, blocks, sums):
+    for b in blocks:
+        base = ref[c, pl.ds(b * SUB, SUB), :]
+        for k in range(LAGS):
+            term = base * ref[c, pl.ds(b * SUB + k, SUB), :]
+            sums[k] = term if sums[k] is None else sums[k] + term
+    return sums
+
+
+def halve(ref, c, start, count):
+    even = ref[c, pl.ds(start, count, stride=2), :]
+    odd = ref[c, pl.ds(start + 1, count, stride=2), :]
+    return (even + odd) * 0.5
+
+
+def kernel(n, frames, x_hbm, lab_ref, val_ref, out_ref, *scratch):
+    it = iter(scratch)
+    x, wt = next(it), next(it)
+    series = [next(it) for _ in range(LOCAL + 1)]
+    far = [next(it) for _ in range(LEVELS - LOCAL)]
+    keepers, partial, landed, result = next(it), next(it), next(it), next(it)
+    load_sem, halo_send, halo_recv = next(it), next(it), next(it)
+    a2a_send, a2a_recv, rs_send, rs_recv, out_send, out_recv = (next(it) for _ in range(6))
+    me = lax.axis_index("tm")
+    rows_out = LEVELS * LAGS // n
+    total = n * frames
+    groups = x.shape[1] // 256
+    top = LOCAL * LAGS
+
+    loads = [
+        pltpu.make_async_copy(
+            x_hbm.at[:, pl.ds(g * 256, 256)], x.at[:, pl.ds(g * 256, 256)], load_sem.at[g]
+        )
+        for g in range(groups)
+    ]
+    for copy in loads:
+        copy.start()
+
+    barrier = pltpu.get_barrier_semaphore()
+
+    @pl.loop(1, n)
+    def _(d):
+        pl.semaphore_signal(
+            barrier, inc=1, device_id={"tm": lax.rem(me + d, n)}, device_id_type=pl.DeviceIdType.MESH
+        )
+
+    cycle = lax.broadcasted_iota(jnp.int32, (Q, 256), 0)
+    for g in range(groups):
+        lab = lab_ref[:, pl.ds(g * 256, 256)]
+        val = val_ref[:, pl.ds(g * 256, 256)].astype(jnp.float32)
+        wt[g] = jnp.where(lab == cycle, val, 0.0).astype(jnp.bfloat16)
+    ones = jnp.ones((16, 256), jnp.bfloat16)
+    acc = jnp.zeros((3 * frames + 16, Q), jnp.float32)
+    for g in range(groups):
+        loads[g].wait()
+        lhs = jnp.concatenate([*split3(x[:, pl.ds(g * 256, 256)]), ones], axis=0)
+        acc = acc + lax.dot_general(
+            lhs, wt[g], (((1,), (1,)), ((), ())), preferred_element_type=jnp.float32
+        )
+    cycle_sum = acc[:frames] + acc[frames : 2 * frames] + acc[2 * frames : 3 * frames]
+    inverse = acc[3 * frames : 3 * frames + 1] / cycle_sum
+    lhs = jnp.concatenate(split3(inverse), axis=0)
+    for g in range(groups):
+        parts = jnp.dot(lhs, wt[g], preferred_element_type=jnp.float32)
+        scale = parts[:frames] + parts[frames : 2 * frames] + parts[2 * frames :]
+        normed = x[:, pl.ds(g * 256, 256)] * scale
+        series[0][2 * g, pl.ds(0, frames), :] = normed[:, :LANES]
+        series[0][2 * g + 1, pl.ds(0, frames), :] = normed[:, LANES:]
+
+    def coarse(c, carry):
+        for l in range(1, LOCAL + 1):
+            series[l][c, pl.ds(0, frames >> l), :] = halve(series[l - 1], c, 0, frames >> l)
+        return carry
+
+    lax.fori_loop(0, n, coarse, 0)
+
+    pl.semaphore_wait(barrier, n - 1)
+
+    def halo(l):
+        first = 0 if l == 0 else SUB
+        count = 2 * SUB - first
+        return pltpu.make_async_remote_copy(
+            src_ref=series[l].at[:, pl.ds(first, count), :],
+            dst_ref=series[l].at[:, pl.ds((frames >> l) + first, count), :],
+            send_sem=halo_send.at[l],
+            recv_sem=halo_recv.at[l],
+            device_id={"tm": lax.rem(me + n - 1, n)},
+            device_id_type=pl.DeviceIdType.MESH,
+        )
+
+    @pl.when(me > 0)
+    def _():
+        for l in range(LOCAL):
+            halo(l).start()
+
+    @pl.when(me == n - 1)
+    def _():
+        for l in range(LOCAL):
+            first = 0 if l == 0 else SUB
+            series[l][:, pl.ds((frames >> l) + first, 2 * SUB - first), :] = jnp.zeros(
+                (n, 2 * SUB - first, LANES), jnp.float32
+            )
+
+    deep = frames >> LOCAL
+
+    def spread(peer, source):
+        return pltpu.make_async_remote_copy(
+            src_ref=series[LOCAL].at[peer],
+            dst_ref=far[0].at[0, pl.ds(pl.multiple_of(source * deep, SUB), deep), :],
+            send_sem=a2a_send.at[peer],
+            recv_sem=a2a_recv.at[source],
+            device_id={"tm": peer},
+            device_id_type=pl.DeviceIdType.MESH,
+        )
+
+    @pl.loop(1, n)
+    def _(d):
+        spread(lax.rem(me + d, n), me).start()
+
+    def inside(c, carry):
+        for l in range(LOCAL):
+            sums = add_lags(series[l], c, range((frames >> l) // SUB - 2), [None] * LAGS)
+            for k in range(LAGS):
+                keepers[c, l * LAGS + k] = sums[k]
+        return carry
+
+    lax.fori_loop(0, n, inside, 0)
+
+    @pl.when(me < n - 1)
+    def _():
+        for l in range(LOCAL):
+            halo(l).wait_recv()
+
+    def reduce_to(peer, source):
+        return pltpu.make_async_remote_copy(
+            src_ref=partial.at[peer],
+            dst_ref=landed.at[source],
+            send_sem=rs_send.at[peer],
+            recv_sem=rs_recv.at[source],
+            device_id={"tm": peer},
+            device_id_type=pl.DeviceIdType.MESH,
+        )
+
+    def edge(c):
+        for l in range(LOCAL):
+            here = frames >> l
+            if l > 0:
+                series[l][c, pl.ds(here, SUB), :] = halve(series[l - 1], c, 2 * here, SUB)
+            sums = [keepers[c, l * LAGS + k] for k in range(LAGS)]
+            sums = add_lags(series[l], c, range(here // SUB - 2, here // SUB), sums)
+            for h in range(LAGS // SUB):
+                partial[c, pl.ds(l * LAGS + h * SUB, SUB), :] = fold_rows(sums[h * SUB : (h + 1) * SUB])
+
+    @pl.loop(1, n)
+    def _(d):
+        peer = lax.rem(me + d, n)
+        edge(peer)
+        reduce_to(peer, me).start()
+
+    edge(me)
+
+    far[0][0, pl.ds(pl.multiple_of(me * deep, SUB), deep), :] = series[LOCAL][me]
+    for i in range(LEVELS - LOCAL):
+        count = total >> (LOCAL + i)
+        far[i][0, pl.ds(count, 2 * SUB), :] = jnp.zeros((2 * SUB, LANES), jnp.float32)
+
+    @pl.loop(1, n)
+    def _(d):
+        spread(me, lax.rem(me + n - d, n)).wait_recv()
+
+    lag = lax.broadcasted_iota(jnp.int32, (SUB, LANES), 0)
+
+    def weight(l, h):
+        return 1.0 / ((total >> l) - h * SUB - lag).astype(jnp.float32)
+
+    for i in range(LEVELS - LOCAL):
+        l = LOCAL + i
+        count = total >> l
+        if i > 0:
+            far[i][0, pl.ds(0, count), :] = halve(far[i - 1], 0, 0, count)
+        sums = add_lags(far[i], 0, range(count // SUB), [None] * LAGS)
+        for h in range(LAGS // SUB):
+            result[pl.ds(l * LAGS + h * SUB, SUB), :] = fold_rows(
+                sums[h * SUB : (h + 1) * SUB]
+            ) * weight(l, h)
+
+    def deliver(peer, source):
+        return pltpu.make_async_remote_copy(
+            src_ref=result.at[pl.ds(pl.multiple_of(peer * rows_out, SUB), rows_out), :],
+            dst_ref=out_ref.at[:, pl.ds(pl.multiple_of(source * LANES, LANES), LANES)],
+            send_sem=out_send.at[peer],
+            recv_sem=out_recv.at[source],
+            device_id={"tm": peer},
+            device_id_type=pl.DeviceIdType.MESH,
+        )
+
+    split = top // rows_out
+
+    @pl.loop(0, n)
+    def _(d):
+        peer = lax.rem(me + d, n)
+
+        @pl.when((peer >= split) & (peer != me))
+        def _():
+            deliver(peer, me).start()
+
+    sums = [partial[me, pl.ds(r * SUB, SUB), :] for r in range(top // SUB)]
+
+    def gather(d, sums):
+        source = lax.rem(me + n - d, n)
+        reduce_to(me, source).wait_recv()
+        return tuple(s + landed[source, pl.ds(r * SUB, SUB), :] for r, s in enumerate(sums))
+
+    sums = lax.fori_loop(1, n, gather, tuple(sums))
+    for r in range(top // SUB):
+        result[pl.ds(r * SUB, SUB), :] = sums[r] * weight(r * SUB // LAGS, r % (LAGS // SUB))
+
+    @pl.loop(0, n)
+    def _(d):
+        peer = lax.rem(me + d, n)
+
+        @pl.when((peer < split) & (peer != me))
+        def _():
+            deliver(peer, me).start()
+
+    out_ref[:, pl.ds(pl.multiple_of(me * LANES, LANES), LANES)] = result[
+        pl.ds(pl.multiple_of(me * rows_out, SUB), rows_out), :
+    ]
+
+    @pl.loop(1, n)
+    def _(d):
+        peer = lax.rem(me + d, n)
+        deliver(me, lax.rem(me + n - d, n)).wait_recv()
+        deliver(peer, me).wait_send()
+        reduce_to(peer, me).wait_send()
+        spread(peer, me).wait_send()
+
+    @pl.when(me > 0)
+    def _():
+        for l in range(LOCAL):
+            halo(l).wait_send()
+
+
+def kernel_body(n, intensity, cycle_label, valid_mask):
+    frames, pixels = intensity.shape
+    f32 = jnp.float32
+    dma = pltpu.SemaphoreType.DMA
+    scratch = [
+        pltpu.VMEM((frames, pixels), f32),
+        pltpu.VMEM((pixels // 256, Q, 256), jnp.bfloat16),
+    ]
+    scratch += [pltpu.VMEM((n, (frames >> l) + 2 * SUB, LANES), f32) for l in range(LOCAL)]
+    scratch += [pltpu.VMEM((n, frames >> LOCAL, LANES), f32)]
+    scratch += [
+        pltpu.VMEM((1, (n * frames >> l) + 2 * SUB, LANES), f32) for l in range(LOCAL, LEVELS)
+    ]
+    scratch += [
+        pltpu.VMEM((n, LOCAL * LAGS, SUB, LANES), f32),
+        pltpu.VMEM((n, LOCAL * LAGS, LANES), f32),
+        pltpu.VMEM((n, LOCAL * LAGS, LANES), f32),
+        pltpu.VMEM((LEVELS * LAGS, LANES), f32),
+        dma((pixels // 256,)),
+        dma((LOCAL,)),
+        dma((LOCAL,)),
+    ] + [dma((n,))] * 6
+    vmem = pl.BlockSpec(memory_space=pltpu.VMEM)
+    return pl.pallas_call(
+        functools.partial(kernel, n, frames),
+        out_shape=jax.ShapeDtypeStruct((LEVELS * LAGS // n, pixels), f32),
+        in_specs=[pl.BlockSpec(memory_space=pl.ANY), vmem, vmem],
+        out_specs=vmem,
+        scratch_shapes=scratch,
+        compiler_params=pltpu.CompilerParams(collective_id=0, has_side_effects=True),
+        name="multitau",
+    )(intensity, cycle_label.reshape(1, pixels), valid_mask.reshape(1, pixels))
+
+
+def route(intensity, cycle_label, valid_mask):
+    n = lax.axis_size("tm")
+    frames, pixels = intensity.shape
+    fits = (
+        lax.axis_size("pix") == 1
+        and pixels == n * LANES
+        and frames == SUB << (LEVELS - 1 - LOCAL)
+        and (LEVELS * LAGS) % (n * SUB) == 0
+    )
+    if fits:
+        return kernel_body(n, intensity, cycle_label, valid_mask)
+    return body(intensity, cycle_label, valid_mask)
+
 
 def solution(mesh):
     placed = (P("tm", ("runs", "pix")), P(("runs", "pix")), P(("runs", "pix")))
     return jax.shard_map(
-        body, mesh=mesh, in_specs=placed, out_specs=P("tm", ("runs", "pix")), check_vma=False
+        route, mesh=mesh, in_specs=placed, out_specs=P("tm", ("runs", "pix")), check_vma=False
     )

time: 95.3 us -> 30 us (0.31)
  other arithmetic: 44.8 us -> 0 us
  blocking collectives: 43.6 us -> 0 us
  Pallas kernels: 0 us -> 28.2 us
  matrix products: 4.86 us -> 0 us
    all_to_all x2 -> x0, blocking collectives: 43.6 us -> none  [the longest x1 31.9 us: body(): lax.all_to_all(pieces, 'tm', split_axis=1, concat_axis=0, tiled=True)]
    reduce_sum x226 -> x0, other arithmetic: 43.6 us -> none  [the longest x119 40.1 us: level_rows(): total = jnp.sum(series[:frames_here - inside] * series[inside:], axis=0)]
    pallas_call x0 -> x1, Pallas kernels: none -> 28.2 us  [kernel_body(): pl.pallas_call(functools.partial(kernel, n, frames), out_shape=jax.ShapeD...]
    dot_general x2 -> x0, matrix products: 4.86 us -> none  [the longest x1 3.63 us: body(): partial_sum = jnp.dot(intensity, weighted, precision=lax.Precision.HIGHEST)]
where the time goes in v1:
time: 30 us; the launch traced here: 29.7 us
  Pallas kernels  28.2 us (94%)
  local copies, waits for them, and re-layouts  1.47 us (5%)
    pallas_call x1, Pallas kernels, kernel_body(): pl.pallas_call(functools.partial(kernel, n, frames), out_shape=jax.ShapeD...  28.2 us
    unnamed x1, local copies, waits for them, and re-layouts  1.47 us

profile of v1, /device:TPU:0, one launch (start us, length us, event | category | flops | bytes accessed | tf_op | source)
XLA Modules:
  0.0 29.7 jit_solution(4860138863709992298)
XLA Ops:
  0.0 28.2 %multitau.1 = f32[8,2048]{1,0:T(8,128)} custom-call(f32[128,2048]{1,0:T(8,128)} %x_hbm.1, s32[1,2048]{1,0:T(1,128)} %bitcast.2, s32[1,2048]{1,0:T(1,128)} %bitcast.3), custom_call_target="tpu_custom_call" | custom-call | tf_op jit(solution)/shard_map/multitau/pallas_call | solution.py:357
  28.2 1.5 %copy.5 = f32[8,2048]{1,0:T(8,128)} copy(f32[8,2048]{1,0:T(8,128)} %multitau.1) | data formatting | bytes 131072

commit v2 on v1

--- a/solution.py
+++ b/solution.py
@@ -58,7 +58,8 @@
     rows_local = pixel_rows(lax.all_to_all(pieces, "tm", split_axis=1, concat_axis=0, tiled=True))
     return lax.all_to_all(rows_local, "tm", split_axis=0, concat_axis=1, tiled=True)
 
-LOCAL = 3
+LOCAL = 2
+CHUNKS = 4
 LANES = 128
 SUB = 8
 
@@ -108,14 +109,14 @@
     x, wt = next(it), next(it)
     series = [next(it) for _ in range(LOCAL + 1)]
     far = [next(it) for _ in range(LEVELS - LOCAL)]
-    keepers, partial, landed, result = next(it), next(it), next(it), next(it)
+    keepers, partial, inbox0, inbox, result = (next(it) for _ in range(5))
     load_sem, halo_send, halo_recv = next(it), next(it), next(it)
-    a2a_send, a2a_recv, rs_send, rs_recv, out_send, out_recv = (next(it) for _ in range(6))
+    hop_send, hop_recv, a2a_send, a2a_recv, out_send, out_recv = (next(it) for _ in range(6))
     me = lax.axis_index("tm")
     rows_out = LEVELS * LAGS // n
     total = n * frames
     groups = x.shape[1] // 256
-    top = LOCAL * LAGS
+    keep = LOCAL * LAGS // rows_out
 
     loads = [
         pltpu.make_async_copy(
@@ -205,7 +206,7 @@
 
     @pl.loop(1, n)
     def _(d):
-        spread(lax.rem(me + d, n), me).start()
+        spread(lax.rem(me + n - d, n), me).start()
 
     def inside(c, carry):
         for l in range(LOCAL):
@@ -221,17 +222,39 @@
         for l in range(LOCAL):
             halo(l).wait_recv()
 
-    def reduce_to(peer, source):
+    side, level = lax.rem(me, 2), lax.rem(me // 2, 2)
+    block = n // CHUNKS
+    stages = [1, 2]
+    while 2 * stages[-1] < n:
+        stages.append(2 * stages[-1])
+
+    def hop(s, q):
+        b = stages[s]
+        part = pl.ds(q * block, block)
+        if s == 0:
+            src, dst = partial.at[1 - side, :, part], inbox0.at[:, part]
+        elif s == 1:
+            src, dst = partial.at[side, 1 - level, part], inbox.at[0, part]
+        else:
+            src, dst = partial.at[side, level, part], inbox.at[s - 1, part]
+        target = me + b - 2 * b * lax.rem(me // b, 2) if s < 2 else lax.rem(me + n - b, n)
         return pltpu.make_async_remote_copy(
-            src_ref=partial.at[peer],
-            dst_ref=landed.at[source],
-            send_sem=rs_send.at[peer],
-            recv_sem=rs_recv.at[source],
-            device_id={"tm": peer},
+            src_ref=src,
+            dst_ref=dst,
+            send_sem=hop_send.at[s, q],
+            recv_sem=hop_recv.at[s, q],
+            device_id={"tm": target},
             device_id_type=pl.DeviceIdType.MESH,
         )
 
-    def edge(c):
+    def sends(s):
+        b = stages[s]
+        return (lax.rem(me, 2 * b) >= b) & (lax.rem(me, b) < 4)
+
+    def receives(s):
+        return lax.rem(me, 2 * stages[s]) < 4
+
+    def edge(c, carry):
         for l in range(LOCAL):
             here = frames >> l
             if l > 0:
@@ -239,15 +262,25 @@
             sums = [keepers[c, l * LAGS + k] for k in range(LAGS)]
             sums = add_lags(series[l], c, range(here // SUB - 2, here // SUB), sums)
             for h in range(LAGS // SUB):
-                partial[c, pl.ds(l * LAGS + h * SUB, SUB), :] = fold_rows(sums[h * SUB : (h + 1) * SUB])
-
-    @pl.loop(1, n)
-    def _(d):
-        peer = lax.rem(me + d, n)
-        edge(peer)
-        reduce_to(peer, me).start()
-
-    edge(me)
+                partial[h, l, c] = fold_rows(sums[h * SUB : (h + 1) * SUB])
+        return carry
+
+    for q in range(CHUNKS):
+        lax.fori_loop(q * block, (q + 1) * block, edge, 0)
+        hop(0, q).start()
+    for q in range(CHUNKS):
+        part = pl.ds(q * block, block)
+        hop(0, q).wait_recv()
+        partial[side, :, part] = partial[side, :, part] + inbox0[:, part]
+        hop(1, q).start()
+    for q in range(CHUNKS):
+        part = pl.ds(q * block, block)
+        hop(1, q).wait_recv()
+        partial[side, level, part] = partial[side, level, part] + inbox[0, part]
+
+        @pl.when(sends(2))
+        def _():
+            hop(2, q).start()
 
     far[0][0, pl.ds(pl.multiple_of(me * deep, SUB), deep), :] = series[LOCAL][me]
     for i in range(LEVELS - LOCAL):
@@ -284,46 +317,63 @@
             device_id_type=pl.DeviceIdType.MESH,
         )
 
-    split = top // rows_out
-
-    @pl.loop(0, n)
+    @pl.loop(1, n)
     def _(d):
-        peer = lax.rem(me + d, n)
-
-        @pl.when((peer >= split) & (peer != me))
+        peer = lax.rem(me + n - d, n)
+
+        @pl.when(peer >= keep)
         def _():
             deliver(peer, me).start()
 
-    sums = [partial[me, pl.ds(r * SUB, SUB), :] for r in range(top // SUB)]
-
-    def gather(d, sums):
-        source = lax.rem(me + n - d, n)
-        reduce_to(me, source).wait_recv()
-        return tuple(s + landed[source, pl.ds(r * SUB, SUB), :] for r, s in enumerate(sums))
-
-    sums = lax.fori_loop(1, n, gather, tuple(sums))
-    for r in range(top // SUB):
-        result[pl.ds(r * SUB, SUB), :] = sums[r] * weight(r * SUB // LAGS, r % (LAGS // SUB))
-
-    @pl.loop(0, n)
-    def _(d):
-        peer = lax.rem(me + d, n)
-
-        @pl.when((peer < split) & (peer != me))
+    for s in range(2, len(stages)):
+
+        @pl.when(receives(s))
         def _():
-            deliver(peer, me).start()
-
-    out_ref[:, pl.ds(pl.multiple_of(me * LANES, LANES), LANES)] = result[
-        pl.ds(pl.multiple_of(me * rows_out, SUB), rows_out), :
-    ]
+            for q in range(CHUNKS):
+                part = pl.ds(q * block, block)
+                hop(s, q).wait_recv()
+                partial[side, level, part] = partial[side, level, part] + inbox[s - 1, part]
+                if s + 1 < len(stages):
+
+                    @pl.when(sends(s + 1))
+                    def _():
+                        hop(s + 1, q).start()
+
+    @pl.when(me < keep)
+    def _():
+        count = total // (level + 1) - side * SUB
+        scale = 1.0 / (count - lag).astype(jnp.float32)
+        for c in range(n):
+            out_ref[:, pl.ds(c * LANES, LANES)] = partial[side, level, c] * scale
+
+    @pl.when(me >= keep)
+    def _():
+        out_ref[:, pl.ds(pl.multiple_of(me * LANES, LANES), LANES)] = result[
+            pl.ds(pl.multiple_of(me * rows_out, SUB), rows_out), :
+        ]
+
+        @pl.loop(1, n)
+        def _(d):
+            deliver(me, lax.rem(me + n - d, n)).wait_recv()
 
     @pl.loop(1, n)
     def _(d):
-        peer = lax.rem(me + d, n)
-        deliver(me, lax.rem(me + n - d, n)).wait_recv()
-        deliver(peer, me).wait_send()
-        reduce_to(peer, me).wait_send()
+        peer = lax.rem(me + n - d, n)
         spread(peer, me).wait_send()
+
+        @pl.when(peer >= keep)
+        def _():
+            deliver(peer, me).wait_send()
+
+    for q in range(CHUNKS):
+        hop(0, q).wait_send()
+        hop(1, q).wait_send()
+    for s in range(2, len(stages)):
+
+        @pl.when(sends(s))
+        def _():
+            for q in range(CHUNKS):
+                hop(s, q).wait_send()
 
     @pl.when(me > 0)
     def _():
@@ -346,13 +396,16 @@
     ]
     scratch += [
         pltpu.VMEM((n, LOCAL * LAGS, SUB, LANES), f32),
-        pltpu.VMEM((n, LOCAL * LAGS, LANES), f32),
-        pltpu.VMEM((n, LOCAL * LAGS, LANES), f32),
+        pltpu.VMEM((2, 2, n, SUB, LANES), f32),
+        pltpu.VMEM((2, n, SUB, LANES), f32),
+        pltpu.VMEM((n.bit_length() - 2, n, SUB, LANES), f32),
         pltpu.VMEM((LEVELS * LAGS, LANES), f32),
         dma((pixels // 256,)),
         dma((LOCAL,)),
         dma((LOCAL,)),
-    ] + [dma((n,))] * 6
+        dma((n.bit_length() - 1, CHUNKS)),
+        dma((n.bit_length() - 1, CHUNKS)),
+    ] + [dma((n,))] * 4
     vmem = pl.BlockSpec(memory_space=pltpu.VMEM)
     return pl.pallas_call(
         functools.partial(kernel, n, frames),
@@ -371,8 +424,9 @@
     fits = (
         lax.axis_size("pix") == 1
         and pixels == n * LANES
-        and frames == SUB << (LEVELS - 1 - LOCAL)
-        and (LEVELS * LAGS) % (n * SUB) == 0
+        and frames % (SUB << LOCAL) == 0
+        and frames >> LOCAL >= 2 * SUB
+        and LEVELS * LAGS == n * SUB
     )
     if fits:
         return kernel_body(n, intensity, cycle_label, valid_mask)

time: 30 us -> 26.4 us (0.88)
  the two profiles are of different devices: /device:TPU:0 before, /device:TPU:4 now
where the time goes in v2:
time: 26.4 us; the launch traced here: 26.2 us
  Pallas kernels  24.7 us (94%)
  local copies, waits for them, and re-layouts  1.47 us (6%)
    pallas_call x1, Pallas kernels, kernel_body(): pl.pallas_call(functools.partial(kernel, n, frames), out_shape=jax.ShapeD...  24.7 us
    unnamed x1, local copies, waits for them, and re-layouts  1.47 us

profile of v2, /device:TPU:4, one launch (start us, length us, event | category | flops | bytes accessed | tf_op | source)
XLA Modules:
  0.0 26.2 jit_solution(16767670460809668352)
XLA Ops:
  0.0 24.7 %multitau.1 = f32[8,2048]{1,0:T(8,128)} custom-call(f32[128,2048]{1,0:T(8,128)} %x_hbm.1, s32[1,2048]{1,0:T(1,128)} %bitcast.2, s32[1,2048]{1,0:T(1,128)} %bitcast.3), custom_call_target="tpu_custom_call" | custom-call | tf_op jit(solution)/shard_map/multitau/pallas_call | solution.py:410
  24.7 1.5 %copy.5 = f32[8,2048]{1,0:T(8,128)} copy(f32[8,2048]{1,0:T(8,128)} %multitau.1) | data formatting | bytes 131072

commit v3 on v2

--- a/solution.py
+++ b/solution.py
@@ -167,22 +167,25 @@
 
     pl.semaphore_wait(barrier, n - 1)
 
-    def halo(l):
+    block = n // CHUNKS
+
+    def halo(l, q):
         first = 0 if l == 0 else SUB
         count = 2 * SUB - first
         return pltpu.make_async_remote_copy(
-            src_ref=series[l].at[:, pl.ds(first, count), :],
-            dst_ref=series[l].at[:, pl.ds((frames >> l) + first, count), :],
-            send_sem=halo_send.at[l],
-            recv_sem=halo_recv.at[l],
+            src_ref=series[l].at[pl.ds(q * block, block), pl.ds(first, count), :],
+            dst_ref=series[l].at[pl.ds(q * block, block), pl.ds((frames >> l) + first, count), :],
+            send_sem=halo_send.at[l, q],
+            recv_sem=halo_recv.at[l, q],
             device_id={"tm": lax.rem(me + n - 1, n)},
             device_id_type=pl.DeviceIdType.MESH,
         )
 
     @pl.when(me > 0)
     def _():
-        for l in range(LOCAL):
-            halo(l).start()
+        for q in range(CHUNKS):
+            for l in range(LOCAL):
+                halo(l, q).start()
 
     @pl.when(me == n - 1)
     def _():
@@ -206,7 +209,7 @@
 
     @pl.loop(1, n)
     def _(d):
-        spread(lax.rem(me + n - d, n), me).start()
+        spread(lax.rem(me + d, n), me).start()
 
     def inside(c, carry):
         for l in range(LOCAL):
@@ -217,13 +220,7 @@
 
     lax.fori_loop(0, n, inside, 0)
 
-    @pl.when(me < n - 1)
-    def _():
-        for l in range(LOCAL):
-            halo(l).wait_recv()
-
     side, level = lax.rem(me, 2), lax.rem(me // 2, 2)
-    block = n // CHUNKS
     stages = [1, 2]
     while 2 * stages[-1] < n:
         stages.append(2 * stages[-1])
@@ -266,6 +263,12 @@
         return carry
 
     for q in range(CHUNKS):
+
+        @pl.when(me < n - 1)
+        def _():
+            for l in range(LOCAL):
+                halo(l, q).wait_recv()
+
         lax.fori_loop(q * block, (q + 1) * block, edge, 0)
         hop(0, q).start()
     for q in range(CHUNKS):
@@ -319,7 +322,7 @@
 
     @pl.loop(1, n)
     def _(d):
-        peer = lax.rem(me + n - d, n)
+        peer = lax.rem(me + d, n)
 
         @pl.when(peer >= keep)
         def _():
@@ -378,7 +381,8 @@
     @pl.when(me > 0)
     def _():
         for l in range(LOCAL):
-            halo(l).wait_send()
+            for q in range(CHUNKS):
+                halo(l, q).wait_send()
 
 
 def kernel_body(n, intensity, cycle_label, valid_mask):
@@ -401,8 +405,8 @@
         pltpu.VMEM((n.bit_length() - 2, n, SUB, LANES), f32),
         pltpu.VMEM((LEVELS * LAGS, LANES), f32),
         dma((pixels // 256,)),
-        dma((LOCAL,)),
-        dma((LOCAL,)),
+        dma((LOCAL, CHUNKS)),
+        dma((LOCAL, CHUNKS)),
         dma((n.bit_length() - 1, CHUNKS)),
         dma((n.bit_length() - 1, CHUNKS)),
     ] + [dma((n,))] * 4

time: 26.4 us -> 25.8 us (0.977)
  the two profiles are of different devices: /device:TPU:4 before, /device:TPU:0 now
where the time goes in v3:
time: 25.8 us; the launch traced here: 25.6 us
  Pallas kernels  24.1 us (93%)
  local copies, waits for them, and re-layouts  1.47 us (6%)
    pallas_call x1, Pallas kernels, kernel_body(): pl.pallas_call(functools.partial(kernel, n, frames), out_shape=jax.ShapeD...  24.1 us
    unnamed x1, local copies, waits for them, and re-layouts  1.47 us

profile of v3, /device:TPU:0, one launch (start us, length us, event | category | flops | bytes accessed | tf_op | source)
XLA Modules:
  0.0 25.6 jit_solution(10393474842496936109)
XLA Ops:
  0.0 24.1 %multitau.1 = f32[8,2048]{1,0:T(8,128)} custom-call(f32[128,2048]{1,0:T(8,128)} %x_hbm.1, s32[1,2048]{1,0:T(1,128)} %bitcast.2, s32[1,2048]{1,0:T(1,128)} %bitcast.3), custom_call_target="tpu_custom_call" | custom-call | tf_op jit(solution)/shard_map/multitau/pallas_call | solution.py:414
  24.1 1.5 %copy.5 = f32[8,2048]{1,0:T(8,128)} copy(f32[8,2048]{1,0:T(8,128)} %multitau.1) | data formatting | bytes 131072
